TPU v7x, 32 devices: a whole 2x2x4 slice. The times are simulated.
32 devices in a mesh: groups: 2 (over x), ctx: 16 (over z, y, core).
Axes of the slice: x: 2, y: 2, z: 4, core: 2. Of those that a mesh axis runs over, the one named last changes fastest.
Arguments:
- queries: bfloat16 [8192, 2560], P(('groups', 'ctx')), parts along dimension 0, may hold values from -6 to 6
- keys: bfloat16 [8192, 2560], P(('groups', 'ctx')), parts along dimension 0, may hold values from -6 to 6
- values: bfloat16 [8192, 2560], P(('groups', 'ctx')), parts along dimension 0, may hold values from -6 to 6
- kv_lists: int32 [16, 4, 2, 8], P('ctx'), may hold values from 0 to 7, as said below
- kv_counts: int32 [16, 4, 2], P('ctx'), may hold values from 0 to 8, as said below
Outputs:
- attended: bfloat16 [8192, 2560], P(('groups', 'ctx')), parts along dimension 0
There are 2 independent parts, one for each index of `groups`. A program takes and returns all parts, laid end to end along the dimension named above; an argument that names none is the same for every part. Nothing has to cross between parts.
Inputs may be any that keep to these rules, and one draw needn't show every extreme that they name: For every device d, level k and side s, the first 8 // 2**k entries of kv_lists[d, k, s] are distinct block indices; later entries are never read. kv_counts[d, k, s] is at most 8 // 2**k and reaches it for some device at every level and side; it is 0 exactly where the partner d - 2**k (s = 0) or d + 2**k (s = 1) lies outside 0 to 15, else 1 or more.
All inputs are finite; a program needn't handle non-finite values.
Results may differ from a plain program's by a relative error of at most 0.005.
Values may be sent and summed in bfloat16 or wider, within the bound.
A program may use at most 128 MiB of HBM per device.

v0:
```python
import math

import jax
import jax.numpy as jnp
from jax import lax
from jax.sharding import PartitionSpec as P

HEAD = 128


masked_score = -1e30


def from_behind(block, axis, distance):
    devices = range(lax.axis_size(axis))
    route = [(i - distance, i) for i in devices if i - distance in devices]
    return lax.ppermute(block, axis, route)


def attend(carried, query_heads, key_rows, value_rows, allowed):
    best_score, weight_total, weighted = carried
    head_count = query_heads.shape[1]
    head_size = query_heads.shape[2]
    key_heads = key_rows.reshape(key_rows.shape[0], head_count, head_size)
    value_heads = value_rows.reshape(value_rows.shape[0], head_count, head_size)
    scores = jnp.einsum(
        "qhd,khd->hqk", query_heads, key_heads, preferred_element_type=jnp.float32
    ) * (1.0 / math.sqrt(head_size))
    if allowed is not None:
        scores = jnp.where(allowed[None, None, :], scores, masked_score)
    fresh_best = jnp.maximum(best_score, jnp.max(scores, axis=-1))
    weights = jnp.exp(scores - fresh_best[:, :, None])
    factor = jnp.exp(best_score - fresh_best)
    weight_total = weight_total * factor + jnp.sum(weights, axis=-1)
    mixed_values = jnp.einsum(
        "hqk,khd->qhd",
        weights.astype(jnp.bfloat16),
        value_heads,
        preferred_element_type=jnp.float32,
    )
    weighted = weighted * jnp.transpose(factor)[:, :, None] + mixed_values
    return (fresh_best, weight_total, weighted)


def shards(queries, keys, values, kv_lists, kv_counts):
    row_count = queries.shape[0]
    width = queries.shape[1]
    head_count = width // HEAD
    block_count = kv_lists.shape[3]
    level_count = kv_lists.shape[1]
    block_rows = row_count // block_count
    query_heads = queries.reshape(row_count, head_count, HEAD)
    carried = (
        jnp.full((head_count, row_count), masked_score, jnp.float32),
        jnp.zeros((head_count, row_count), jnp.float32),
        jnp.zeros((row_count, head_count, HEAD), jnp.float32),
    )
    carried = attend(carried, query_heads, keys, values, None)
    key_blocks = keys.reshape(block_count, block_rows, width)
    value_blocks = values.reshape(block_count, block_rows, width)
    every_list = lax.all_gather(kv_lists, "ctx", axis=0, tiled=True)
    here_index = lax.axis_index("ctx")
    ctx_count = lax.axis_size("ctx")
    for level_id in range(level_count):
        distance = 1 << level_id
        capacity = block_count >> level_id
        for side_id in range(2):
            offset = distance if side_id == 0 else -distance
            counted = kv_counts[0, level_id, side_id]
            allowed = jnp.arange(capacity * block_rows, dtype=jnp.int32) // block_rows < counted
            target = jnp.clip(here_index + offset, 0, ctx_count - 1)
            wanted = lax.dynamic_index_in_dim(every_list, target, 0, keepdims=False)[
                level_id, side_id, :capacity
            ]
            packed = jnp.stack(
                [jnp.take(key_blocks, wanted, axis=0), jnp.take(value_blocks, wanted, axis=0)]
            )
            arrived = from_behind(packed, "ctx", offset)
            far_keys = arrived[0]
            far_values = arrived[1]
            carried = attend(
                carried,
                query_heads,
                far_keys.reshape(capacity * block_rows, width),
                far_values.reshape(capacity * block_rows, width),
                allowed,
            )
    best_score, weight_total, weighted = carried
    result = weighted / jnp.transpose(weight_total)[:, :, None]
    return result.reshape(row_count, width).astype(jnp.bfloat16)


def solution(mesh):
    in_specs = (
        P(("groups", "ctx"), None),
        P(("groups", "ctx"), None),
        P(("groups", "ctx"), None),
        P("ctx", None, None, None),
        P("ctx", None, None),
    )
    out_specs = P(("groups", "ctx"), None)
    return jax.shard_map(shards, mesh=mesh, in_specs=in_specs, out_specs=out_specs, check_vma=False)
```

profile of v0, /device:TPU:10, one launch (start us, length us, event | category | flops | bytes accessed | tf_op | source)
XLA Modules:
  0.0 219.9 jit_solution(879587065999367864)
XLA Ops:
  0.8 19.0 %all_gather.3 = s32[16,4,2,8]{3,1,2,0:T(4,128)S(1)} all-gather(s32[1,4,2,8]{3,1,2,0:T(4,128)S(1)} %copy.64), channel_id=1, replica_groups=mesh['groups'=2,'ctx'=16] {'ctx'}, dimensions={0}, use_global_device_ids=true | all-gather | bytes 4352 | tf_op jit(solution)/shard_map/all_gather | solution.py:61
  19.8 1.9 gather_fusion.2
  21.8 1.7 gather_fusion.3
  23.5 1.6 select_bitcast_fusion.1
  25.1 1.7 pad_maximum_fusion.1
  26.8 2.4 %collective-permute-start.1 = (bf16[2,8,32,2560]{3,2,1,0:T(8,128)(2,1)}, bf16[2,8,32,2560]{3,2,1,0:T(8,128)(2,1)}, u32[]{:S(2)}, u32[]{:S(2)}) collective-permute-start(bf16[2,8,32,2560]{3,2,1,0:T(8,128)(2,1)} %pad_maximum_fusion.1), channel_id=1, source_target_pairs={{1,0},{2,1},{3,2},{4,3},{5,4},{6,5},{7,6},{8,7},{9,8},{10,9},{11,1... | collective-permute-start | bytes 7864328 | tf_op jit(solution)/shard_map/ppermute | solution.py:17
  29.2 1.7 gather_fusion
  30.9 1.7 gather_fusion.1
  32.6 2.0 select_bitcast_fusion.3
  34.6 1.8 pad_maximum_fusion
  36.5 2.0 collective-permute-start
  42.9 6.1 %collective-permute-start.3 = (bf16[2,4,32,2560]{3,2,1,0:T(8,128)(2,1)}, bf16[2,4,32,2560]{3,2,1,0:T(8,128)(2,1)}, u32[]{:S(2)}, u32[]{:S(2)}) collective-permute-start(bf16[2,4,32,2560]{3,2,1,0:T(8,128)(2,1)} %pad_maximum_fusion.3), channel_id=1, source_target_pairs={{2,0},{3,1},{4,2},{5,3},{6,4},{7,5},{8,6},{9,7},{10,8},{11,9},{12,... | collective-permute-start | bytes 3932168 | tf_op jit(solution)/shard_map/ppermute | solution.py:17
  53.5 1.9 collective-permute-start.2
  70.7 1.6 copy.58
  72.3 1.8 broadcast_compare_fusion
  79.9 3.2 %multiply_reduce_fusion = (f32[20,256]{1,0:T(8,128)S(1)}, f32[20,256,256]{1,2,0:T(8,128)}) fusion(bf16[256,20,128]{0,2,1:T(8,128)(2,1)S(1)} %bitcast.392, bf16[256,20,128]{0,2,1:T(8,128)(2,1)S(1)} %bitcast.417), kind=kOutput, calls=%fused_computation.21 | convolution fusion | flops 338160640 | bytes 7884800 | tf_op jit(solution)/shard_map/qhd,khd->hqk/dot_general | solution.py:26
  83.2 11.3 %collective-permute-done.7 = bf16[2,1,32,2560]{3,2,1,0:T(8,128)(2,1)} collective-permute-done((bf16[2,1,32,2560]{3,2,1,0:T(8,128)(2,1)}, bf16[2,1,32,2560]{3,2,1,0:T(8,128)(2,1)}, u32[]{:S(2)}, u32[]{:S(2)}) %collective-permute-start.7) | collective-permute-done | bytes 327712 | tf_op jit(solution)/shard_map/ppermute | solution.py:17
  96.9 3.5 %collective-permute-done.6 = bf16[2,1,32,2560]{3,2,1,0:T(8,128)(2,1)S(1)} collective-permute-done((bf16[2,1,32,2560]{3,2,1,0:T(8,128)(2,1)S(1)}, bf16[2,1,32,2560]{3,2,1,0:T(8,128)(2,1)S(1)}, u32[]{:S(2)}, u32[]{:S(2)}) %collective-permute-start.6) | collective-permute-done | bytes 327712 | tf_op jit(solution)/shard_map/ppermute | solution.py:17
  100.5 9.0 %collective-permute-start.5 = (bf16[2,2,32,2560]{3,2,1,0:T(8,128)(2,1)}, bf16[2,2,32,2560]{3,2,1,0:T(8,128)(2,1)}, u32[]{:S(2)}, u32[]{:S(2)}) collective-permute-start(bf16[2,2,32,2560]{3,2,1,0:T(8,128)(2,1)} %pad_maximum_fusion.5), channel_id=1, source_target_pairs={{4,0},{5,1},{6,2},{7,3},{8,4},{9,5},{10,6},{11,7},{12,8},{13,9},{1... | collective-permute-start | bytes 1966088 | tf_op jit(solution)/shard_map/ppermute | solution.py:17
  111.6 1.8 fusion.134
  113.4 6.9 %collective-permute-done.5 = bf16[2,2,32,2560]{3,2,1,0:T(8,128)(2,1)} collective-permute-done((bf16[2,2,32,2560]{3,2,1,0:T(8,128)(2,1)}, bf16[2,2,32,2560]{3,2,1,0:T(8,128)(2,1)}, u32[]{:S(2)}, u32[]{:S(2)}) %collective-permute-start.5) | collective-permute-done | bytes 655392 | tf_op jit(solution)/shard_map/ppermute | solution.py:17
  120.3 3.9 %collective-permute-start.4 = (bf16[2,2,32,2560]{3,2,1,0:T(8,128)(2,1)}, bf16[2,2,32,2560]{3,2,1,0:T(8,128)(2,1)}, u32[]{:S(2)}, u32[]{:S(2)}) collective-permute-start(bf16[2,2,32,2560]{3,2,1,0:T(8,128)(2,1)} %pad_maximum_fusion.4), channel_id=1, source_target_pairs={{0,4},{1,5},{2,6},{3,7},{4,8},{5,9},{6,10},{7,11},{8,12},{9,13},{1... | collective-permute-start | bytes 1966088 | tf_op jit(solution)/shard_map/ppermute | solution.py:17
  126.3 6.8 %collective-permute-done.4 = bf16[2,2,32,2560]{3,2,1,0:T(8,128)(2,1)} collective-permute-done((bf16[2,2,32,2560]{3,2,1,0:T(8,128)(2,1)}, bf16[2,2,32,2560]{3,2,1,0:T(8,128)(2,1)}, u32[]{:S(2)}, u32[]{:S(2)}) %collective-permute-start.4) | collective-permute-done | bytes 655392 | tf_op jit(solution)/shard_map/ppermute | solution.py:17
  137.0 2.0 fusion.135
  139.1 2.0 fusion.136
  141.1 3.8 %collective-permute-done.3 = bf16[2,4,32,2560]{3,2,1,0:T(8,128)(2,1)} collective-permute-done((bf16[2,4,32,2560]{3,2,1,0:T(8,128)(2,1)}, bf16[2,4,32,2560]{3,2,1,0:T(8,128)(2,1)}, u32[]{:S(2)}, u32[]{:S(2)}) %collective-permute-start.3) | collective-permute-done | bytes 1310752 | tf_op jit(solution)/shard_map/ppermute | solution.py:17
  144.9 2.5 %fusion.127 = (bf16[1,4,32,2560]{3,2,1,0:T(8,128)(2,1)}, bf16[1,4,32,2560]{3,2,1,0:T(8,128)(2,1)}) fusion(bf16[2,4,32,2560]{3,2,1,0:T(8,128)(2,1)} %collective-permute-done.3), kind=kLoop, calls=%fused_computation.273 | loop fusion | bytes 2621440 | tf_op jit(solution)/shard_map/slice | solution.py:80
  147.4 2.3 %reshape_reshape_squeeze.54 = bf16[128,20,128]{2,1,0:T(8,128)(2,1)} reshape(bf16[1,4,32,2560]{3,2,1,0:T(8,128)(2,1)} %get-tuple-element.57) | data formatting | bytes 1310720 | tf_op jit(solution)/shard_map/reshape;reshape;squeeze | solution.py:24
  149.7 2.5 %fusion.126 = (bf16[1,4,32,2560]{3,2,1,0:T(8,128)(2,1)}, bf16[1,4,32,2560]{3,2,1,0:T(8,128)(2,1)}) fusion(bf16[2,4,32,2560]{3,2,1,0:T(8,128)(2,1)} %collective-permute-done.2), kind=kLoop, calls=%fused_computation.272 | loop fusion | bytes 2621440 | tf_op jit(solution)/shard_map/slice | solution.py:80
  152.1 2.2 %reshape_reshape_squeeze.52 = bf16[128,20,128]{2,1,0:T(8,128)(2,1)} reshape(bf16[1,4,32,2560]{3,2,1,0:T(8,128)(2,1)} %get-tuple-element.55) | data formatting | bytes 1310720 | tf_op jit(solution)/shard_map/reshape;reshape;squeeze | solution.py:24
  154.4 2.2 %reshape_reshape_squeeze.53 = bf16[128,20,128]{2,1,0:T(8,128)(2,1)} reshape(bf16[1,4,32,2560]{3,2,1,0:T(8,128)(2,1)} %get-tuple-element.54) | data formatting | bytes 1310720 | tf_op jit(solution)/shard_map/reshape;reshape;squeeze | solution.py:25
  156.6 2.2 %reshape_reshape_squeeze.55 = bf16[128,20,128]{2,1,0:T(8,128)(2,1)} reshape(bf16[1,4,32,2560]{3,2,1,0:T(8,128)(2,1)} %get-tuple-element.56) | data formatting | bytes 1310720 | tf_op jit(solution)/shard_map/reshape;reshape;squeeze | solution.py:25
  158.8 3.9 %bitcast_reduce_fusion.2 = (f32[20,256]{1,0:T(8,128)}, f32[20,128,256]{2,1,0:T(8,128)}) fusion(pred[128]{0:T(512)(128)(4,1)S(1)} %get-tuple-element.131, bf16[256,20,128]{0,2,1:T(8,128)(2,1)S(1)} %bitcast.397, bf16[128,20,128]{2,1,0:T(8,128)(2,1)} %reshape_reshape_squeeze.54), kind=kOutput, calls=%fused_computation.45 | convolution fusion | flops 169733120 | bytes 4608128 | tf_op jit(solution)/shard_map/qhd,khd->hqk/dot_general | solution.py:26
  162.7 2.1 bitcast_reduce_fusion.3
  164.8 3.5 %fusion.125 = (bf16[1,8,32,2560]{3,2,1,0:T(8,128)(2,1)}, bf16[1,8,32,2560]{3,2,1,0:T(8,128)(2,1)}) fusion(bf16[2,8,32,2560]{3,2,1,0:T(8,128)(2,1)} %collective-permute-done.1), kind=kLoop, calls=%fused_computation.271 | loop fusion | bytes 5242880 | tf_op jit(solution)/shard_map/slice | solution.py:80
  168.3 3.5 %reshape_reshape_squeeze.50 = bf16[256,20,128]{2,1,0:T(8,128)(2,1)} reshape(bf16[1,8,32,2560]{3,2,1,0:T(8,128)(2,1)} %get-tuple-element.53) | data formatting | bytes 2621440 | tf_op jit(solution)/shard_map/reshape;reshape;squeeze | solution.py:24
  171.8 3.5 %fusion.124 = (bf16[1,8,32,2560]{3,2,1,0:T(8,128)(2,1)}, bf16[1,8,32,2560]{3,2,1,0:T(8,128)(2,1)}) fusion(bf16[2,8,32,2560]{3,2,1,0:T(8,128)(2,1)} %collective-permute-done), kind=kLoop, calls=%fused_computation.270 | loop fusion | bytes 5242880 | tf_op jit(solution)/shard_map/slice | solution.py:80
  175.3 3.5 %reshape_reshape_squeeze.48 = bf16[256,20,128]{2,1,0:T(8,128)(2,1)} reshape(bf16[1,8,32,2560]{3,2,1,0:T(8,128)(2,1)} %get-tuple-element.51) | data formatting | bytes 2621440 | tf_op jit(solution)/shard_map/reshape;reshape;squeeze | solution.py:24
  178.8 3.5 %reshape_reshape_squeeze.49 = bf16[256,20,128]{2,1,0:T(8,128)(2,1)} reshape(bf16[1,8,32,2560]{3,2,1,0:T(8,128)(2,1)} %get-tuple-element.50) | data formatting | bytes 2621440 | tf_op jit(solution)/shard_map/reshape;reshape;squeeze | solution.py:25
  182.3 5.2 %bitcast_reduce_fusion = (f32[20,256]{1,0:T(8,128)S(1)}, f32[20,256,256]{1,2,0:T(8,128)}) fusion(pred[256]{0:T(512)(128)(4,1)S(1)} %get-tuple-element.125, bf16[256,20,128]{0,2,1:T(8,128)(2,1)S(1)} %bitcast.399, bf16[256,20,128]{2,1,0:T(8,128)(2,1)} %reshape_reshape_squeeze.50), kind=kOutput, calls=%fused_computation.13 | convolution fusion | flops 339471360 | bytes 7885056 | tf_op jit(solution)/shard_map/qhd,khd->hqk/dot_general | solution.py:26
  187.6 1.6 bitcast_reduce_fusion.1
  190.6 2.4 %fusion.4 = f32[20,256]{1,0:T(8,128)} fusion(f32[20,256,256]{1,2,0:T(8,128)S(1)} %get-tuple-element.116, f32[20,256]{1,0:T(8,128)S(1)} %get-tuple-element.37, pred[256]{0:T(512)(128)(4,1)S(1)} %copy-done.48), kind=kLoop, calls=%fused_computation.24 | loop fusion | flops 5237760 | bytes 5284096 | tf_op jit(solution)/shard_map/reduce_sum | solution.py:34
  193.0 3.0 %fusion.10 = f32[20,128,256]{2,1,0:T(8,128)} fusion(f32[20,256,256]{1,2,0:T(8,128)S(1)} %get-tuple-element.116, f32[20,256]{1,0:T(8,128)S(1)} %get-tuple-element.37, pred[256]{0:T(512)(128)(4,1)S(1)} %copy-done.48, bf16[256,20,128]{2,1,0:T(8,128)(2,1)S(1)} %copy-done.8), kind=kOutput, calls=%fused_computation.29 | convolution fusion | flops 340787200 | bytes 9195776 | tf_op jit(solution)/shard_map/hqk,khd->qhd/dot_general | solution.py:35
  196.0 1.7 reshape_reshape_squeeze.51
  197.7 3.7 %fusion.6 = f32[20,256]{1,0:T(8,128)S(1)} fusion(f32[20,256,256]{1,2,0:T(8,128)} %get-tuple-element.114, f32[20,256]{1,0:T(8,128)} %get-tuple-element.36, pred[256]{0:T(512)(128)(4,1)} %copy-done.46), kind=kLoop, calls=%fused_computation.26 | loop fusion | flops 5237760 | bytes 5284096 | tf_op jit(solution)/shard_map/reduce_sum | solution.py:34
  201.4 3.9 %fusion.8 = f32[20,128,256]{2,1,0:T(8,128)S(1)} fusion(f32[20,256,256]{1,2,0:T(8,128)} %get-tuple-element.114, f32[20,256]{1,0:T(8,128)S(1)} %copy-done.38, pred[256]{0:T(512)(128)(4,1)S(1)} %copy-done.47, bf16[256,20,128]{2,1,0:T(8,128)(2,1)S(1)} %copy-done.9), kind=kOutput, calls=%fused_computation.28 | convolution fusion | flops 340787200 | bytes 9195776 | tf_op jit(solution)/shard_map/hqk,khd->qhd/dot_general | solution.py:35
  216.1 2.2 fusion.15
  218.3 1.6 copy.101
  (183 shorter events, 49.1 us)
Async XLA Ops:
  0.0 21.8 %copy-start.1 = (bf16[256,2560]{1,0:T(8,128)(2,1)S(1)}, bf16[256,2560]{1,0:T(8,128)(2,1)}, u32[]{:S(2)}) copy-start(bf16[256,2560]{1,0:T(8,128)(2,1)} %param.15) | copy-start | bytes 3932164
  25.1 4.1 %copy-start = (bf16[256,2560]{1,0:T(8,128)(2,1)S(1)}, bf16[256,2560]{1,0:T(8,128)(2,1)}, u32[]{:S(2)}) copy-start(bf16[256,2560]{1,0:T(8,128)(2,1)} %param.14) | copy-start | bytes 3932164
  26.8 137.9 %collective-permute-start.1 = (bf16[2,8,32,2560]{3,2,1,0:T(8,128)(2,1)}, bf16[2,8,32,2560]{3,2,1,0:T(8,128)(2,1)}, u32[]{:S(2)}, u32[]{:S(2)}) collective-permute-start(bf16[2,8,32,2560]{3,2,1,0:T(8,128)(2,1)} %pad_maximum_fusion.1), channel_id=1, source_target_pairs={{1,0},{2,1},{3,2},{4,3},{5,4},{6,5},{7,6},{8,7},{9,8},{10,9},{11,1... | collective-permute-start | bytes 7864328 | tf_op jit(solution)/shard_map/ppermute | solution.py:17
  36.5 135.4 %collective-permute-start = (bf16[2,8,32,2560]{3,2,1,0:T(8,128)(2,1)}, bf16[2,8,32,2560]{3,2,1,0:T(8,128)(2,1)}, u32[]{:S(2)}, u32[]{:S(2)}) collective-permute-start(bf16[2,8,32,2560]{3,2,1,0:T(8,128)(2,1)} %pad_maximum_fusion), channel_id=1, source_target_pairs={{0,1},{1,2},{2,3},{3,4},{4,5},{5,6},{6,7},{7,8},{8,9},{9,10},{10,1... | collective-permute-start | bytes 7864328 | tf_op jit(solution)/shard_map/ppermute | solution.py:17
  42.9 102.0 %collective-permute-start.3 = (bf16[2,4,32,2560]{3,2,1,0:T(8,128)(2,1)}, bf16[2,4,32,2560]{3,2,1,0:T(8,128)(2,1)}, u32[]{:S(2)}, u32[]{:S(2)}) collective-permute-start(bf16[2,4,32,2560]{3,2,1,0:T(8,128)(2,1)} %pad_maximum_fusion.3), channel_id=1, source_target_pairs={{2,0},{3,1},{4,2},{5,3},{6,4},{7,5},{8,6},{9,7},{10,8},{11,9},{12,... | collective-permute-start | bytes 3932168 | tf_op jit(solution)/shard_map/ppermute | solution.py:17
  53.5 96.1 %collective-permute-start.2 = (bf16[2,4,32,2560]{3,2,1,0:T(8,128)(2,1)}, bf16[2,4,32,2560]{3,2,1,0:T(8,128)(2,1)}, u32[]{:S(2)}, u32[]{:S(2)}) collective-permute-start(bf16[2,4,32,2560]{3,2,1,0:T(8,128)(2,1)} %pad_maximum_fusion.2), channel_id=1, source_target_pairs={{0,2},{1,3},{2,4},{3,5},{4,6},{5,7},{6,8},{7,9},{8,10},{9,11},{10,... | collective-permute-start | bytes 3932168 | tf_op jit(solution)/shard_map/ppermute | solution.py:17
  62.0 32.5 %collective-permute-start.7 = (bf16[2,1,32,2560]{3,2,1,0:T(8,128)(2,1)}, bf16[2,1,32,2560]{3,2,1,0:T(8,128)(2,1)}, u32[]{:S(2)}, u32[]{:S(2)}) collective-permute-start(bf16[2,1,32,2560]{3,2,1,0:T(8,128)(2,1)} %pad_maximum_fusion.7), channel_id=1, source_target_pairs={{8,0},{9,1},{10,2},{11,3},{12,4},{13,5},{14,6},{15,7},{24,16},{25,... | collective-permute-start | bytes 983048 | tf_op jit(solution)/shard_map/ppermute | solution.py:17
  67.1 2.9 %copy-start.45 = (s32[1,4,2]{1,2,0:T(2,128)S(1)}, s32[1,4,2]{1,2,0:T(2,128)}, u32[]{:S(2)}) copy-start(s32[1,4,2]{1,2,0:T(2,128)} %param.17) | copy-start | bytes 100
  70.0 5.3 %copy-start.19 = (bf16[2,32,2560]{2,1,0:T(8,128)(2,1)S(1)}, bf16[2,32,2560]{2,1,0:T(8,128)(2,1)}, u32[]{:S(2)}) copy-start(bf16[2,32,2560]{2,1,0:T(8,128)(2,1)} %gather_fusion.10) | copy-start | bytes 983044
  70.0 5.3 %copy-start.20 = (bf16[2,32,2560]{2,1,0:T(8,128)(2,1)S(1)}, bf16[2,32,2560]{2,1,0:T(8,128)(2,1)}, u32[]{:S(2)}) copy-start(bf16[2,32,2560]{2,1,0:T(8,128)(2,1)} %gather_fusion.11) | copy-start | bytes 983044
  74.0 108.3 %copy-start.46 = (pred[256]{0:T(512)(128)(4,1)}, pred[256]{0:T(512)(128)(4,1)S(1)}, u32[]{:S(2)}) copy-start(pred[256]{0:T(512)(128)(4,1)S(1)} %get-tuple-element.125) | copy-start | bytes 772
  75.3 4.6 %copy-start.11 = (bf16[256,2560]{0,1:T(8,128)(2,1)S(1)}, bf16[256,2560]{0,1:T(8,128)(2,1)}, u32[]{:S(2)}) copy-start(bf16[256,2560]{0,1:T(8,128)(2,1)} %copy.59) | copy-start | bytes 3932164
  79.9 3.2 %copy-start.22 = (bf16[1,1,32,2560]{3,2,1,0:T(8,128)(2,1)S(1)}, bf16[1,1,32,2560]{3,2,1,0:T(8,128)(2,1)}, u32[]{:S(2)}) copy-start(bf16[1,1,32,2560]{3,2,1,0:T(8,128)(2,1)} %get-tuple-element.61) | copy-start | bytes 491524
  94.5 6.0 %collective-permute-start.6 = (bf16[2,1,32,2560]{3,2,1,0:T(8,128)(2,1)S(1)}, bf16[2,1,32,2560]{3,2,1,0:T(8,128)(2,1)S(1)}, u32[]{:S(2)}, u32[]{:S(2)}) collective-permute-start(bf16[2,1,32,2560]{3,2,1,0:T(8,128)(2,1)S(1)} %pad_maximum_fusion.6), channel_id=1, source_target_pairs={{0,8},{1,9},{2,10},{3,11},{4,12},{5,13},{6,14},{7,15},{16,24},{17,... | collective-permute-start | bytes 983048 | tf_op jit(solution)/shard_map/ppermute | solution.py:17
  100.5 19.8 %collective-permute-start.5 = (bf16[2,2,32,2560]{3,2,1,0:T(8,128)(2,1)}, bf16[2,2,32,2560]{3,2,1,0:T(8,128)(2,1)}, u32[]{:S(2)}, u32[]{:S(2)}) collective-permute-start(bf16[2,2,32,2560]{3,2,1,0:T(8,128)(2,1)} %pad_maximum_fusion.5), channel_id=1, source_target_pairs={{4,0},{5,1},{6,2},{7,3},{8,4},{9,5},{10,6},{11,7},{12,8},{13,9},{1... | collective-permute-start | bytes 1966088 | tf_op jit(solution)/shard_map/ppermute | solution.py:17
  120.3 12.8 %collective-permute-start.4 = (bf16[2,2,32,2560]{3,2,1,0:T(8,128)(2,1)}, bf16[2,2,32,2560]{3,2,1,0:T(8,128)(2,1)}, u32[]{:S(2)}, u32[]{:S(2)}) collective-permute-start(bf16[2,2,32,2560]{3,2,1,0:T(8,128)(2,1)} %pad_maximum_fusion.4), channel_id=1, source_target_pairs={{0,4},{1,5},{2,6},{3,7},{4,8},{5,9},{6,10},{7,11},{8,12},{9,13},{1... | collective-permute-start | bytes 1966088 | tf_op jit(solution)/shard_map/ppermute | solution.py:17
  137.0 2.0 copy-start.18
  158.8 3.9 %copy-start.15 = (bf16[128,20,128]{2,1,0:T(8,128)(2,1)S(1)}, bf16[128,20,128]{2,1,0:T(8,128)(2,1)}, u32[]{:S(2)}) copy-start(bf16[128,20,128]{2,1,0:T(8,128)(2,1)} %reshape_reshape_squeeze.52) | copy-start | bytes 1966084
  182.3 5.2 %copy-start.7 = (bf16[256,20,128]{2,1,0:T(8,128)(2,1)S(1)}, bf16[256,20,128]{2,1,0:T(8,128)(2,1)}, u32[]{:S(2)}) copy-start(bf16[256,20,128]{2,1,0:T(8,128)(2,1)} %reshape_reshape_squeeze.48) | copy-start | bytes 3932164
  182.3 5.2 %copy-start.48 = (pred[256]{0:T(512)(128)(4,1)S(1)}, pred[256]{0:T(512)(128)(4,1)}, u32[]{:S(2)}) copy-start(pred[256]{0:T(512)(128)(4,1)} %get-tuple-element.126) | copy-start | bytes 772
  187.5 1.7 copy-start.34
  187.5 2.3 %copy-start.25 = (f32[20,256]{1,0:T(8,128)S(1)}, f32[20,256]{1,0:T(8,128)}, u32[]{:S(2)}) copy-start(f32[20,256]{1,0:T(8,128)} %get-tuple-element.101) | copy-start | bytes 61444
  187.5 2.3 %copy-start.27 = (f32[20,256]{1,0:T(8,128)S(1)}, f32[20,256]{1,0:T(8,128)}, u32[]{:S(2)}) copy-start(f32[20,256]{1,0:T(8,128)} %get-tuple-element.103) | copy-start | bytes 61444
  187.5 2.3 %copy-start.29 = (f32[20,256]{1,0:T(8,128)S(1)}, f32[20,256]{1,0:T(8,128)}, u32[]{:S(2)}) copy-start(f32[20,256]{1,0:T(8,128)} %get-tuple-element.105) | copy-start | bytes 61444
  187.5 2.3 %copy-start.31 = (f32[20,256]{1,0:T(8,128)S(1)}, f32[20,256]{1,0:T(8,128)}, u32[]{:S(2)}) copy-start(f32[20,256]{1,0:T(8,128)} %get-tuple-element.107) | copy-start | bytes 61444
  190.6 2.4 %copy-start.8 = (bf16[256,20,128]{2,1,0:T(8,128)(2,1)S(1)}, bf16[256,20,128]{2,1,0:T(8,128)(2,1)}, u32[]{:S(2)}) copy-start(bf16[256,20,128]{2,1,0:T(8,128)(2,1)} %reshape_reshape_squeeze.49) | copy-start | bytes 3932164
  193.0 3.0 %copy-start.10 = (bf16[1,8,32,2560]{3,2,1,0:T(8,128)(2,1)S(1)}, bf16[1,8,32,2560]{3,2,1,0:T(8,128)(2,1)}, u32[]{:S(2)}) copy-start(bf16[1,8,32,2560]{3,2,1,0:T(8,128)(2,1)} %get-tuple-element.52) | copy-start | bytes 3932164
  197.7 3.7 %copy-start.9 = (bf16[256,20,128]{2,1,0:T(8,128)(2,1)S(1)}, bf16[256,20,128]{2,1,0:T(8,128)(2,1)}, u32[]{:S(2)}) copy-start(bf16[256,20,128]{2,1,0:T(8,128)(2,1)} %reshape_reshape_squeeze.51) | copy-start | bytes 3932164
  197.7 3.7 %copy-start.38 = (f32[20,256]{1,0:T(8,128)S(1)}, f32[20,256]{1,0:T(8,128)}, u32[]{:S(2)}) copy-start(f32[20,256]{1,0:T(8,128)} %get-tuple-element.36) | copy-start | bytes 61444
  197.7 3.7 %copy-start.47 = (pred[256]{0:T(512)(128)(4,1)S(1)}, pred[256]{0:T(512)(128)(4,1)}, u32[]{:S(2)}) copy-start(pred[256]{0:T(512)(128)(4,1)} %copy-done.46) | copy-start | bytes 772
  201.4 4.0 %copy-start.3 = (f32[20,128,256]{2,1,0:T(8,128)S(1)}, f32[20,128,256]{2,1,0:T(8,128)}, u32[]{:S(2)}) copy-start(f32[20,128,256]{2,1,0:T(8,128)} %get-tuple-element.112) | copy-start | bytes 7864324
  201.4 4.0 %copy-start.24 = (f32[20,256]{1,0:T(8,128)S(1)}, f32[20,256]{1,0:T(8,128)}, u32[]{:S(2)}) copy-start(f32[20,256]{1,0:T(8,128)} %get-tuple-element.35) | copy-start | bytes 61444
  205.4 1.1 copy-start.14
  205.4 2.0 copy-start.2
  206.5 3.2 %slice-start = ((s8[5242880]{0:T(1024)(128)(4,1)}), s8[4194304]{0:T(1024)(128)(4,1)S(1)}, s32[]{:S(2)}) async-start(s8[5242880]{0:T(1024)(128)(4,1)} %bitcast.401), calls=%async_computation | async-start | bytes 8388608
  207.4 1.5 copy-start.13
  207.4 2.3 %slice-start.1 = ((s8[5242880]{0:T(1024)(128)(4,1)}), s8[1048576]{0:T(1024)(128)(4,1)S(1)}, s32[]{:S(2)}) async-start(s8[5242880]{0:T(1024)(128)(4,1)} %bitcast.401), calls=%async_computation.1 | async-start | bytes 2097152
  209.7 1.3 copy-start.12
  211.1 1.3 copy-start.4
  211.1 1.3 copy-start.36
  211.1 1.5 copy-start.17
  213.2 1.1 copy-start.6
  214.2 1.1 copy-start.26
  214.2 1.1 copy-start.28
  214.2 1.1 copy-start.30
  214.3 1.8 copy-start.5
  214.3 1.8 copy-start.43
  214.3 1.8 copy-start.44
  (11 other events, 11.1 us)
where the time goes:
time: 221 us; the launch traced here: 220 us
  local copies, waits for them, and re-layouts  67.7 us (31%)
  matrix products  36.2 us (16%)
  waiting for transfers between devices  32.4 us (15%)
  other arithmetic  31.7 us (14%)
  starting transfers between devices  27.9 us (13%)
  blocking collectives  19 us (9%)
  between operations  4.86 us (2%)
    ppermute x8, waiting for transfers between devices, from_behind(): return lax.ppermute(block, axis, route)  32.4 us
    ppermute x8, starting transfers between devices, from_behind(): return lax.ppermute(block, axis, route)  27.9 us
    dot_general x9, matrix products, attend(): jnp.einsum('qhd,khd->hqk', query_heads, key_heads, preferred_element_type...  22.7 us
    all_gather x1, blocking collectives, shards(): every_list = lax.all_gather(kv_lists, 'ctx', axis=0, tiled=True)  19 us
    another operation x16, other arithmetic, shards(): jnp.stack([jnp.take(key_blocks, wanted, axis=0), jnp.take(value_blocks, w...  15.7 us
    slice x8, local copies, waits for them, and re-layouts, shards(): far_values = arrived[1]  15.3 us
    another operation x8, local copies, waits for them, and re-layouts, attend(): key_heads = key_rows.reshape(key_rows.shape[0], head_count, head_size)  13.6 us
    dot_general x9, matrix products, attend(): jnp.einsum('hqk,khd->qhd', weights.astype(jnp.bfloat16), value_heads, pre...  13.5 us
  transfers between devices with their start and end apart: 8, of which 5 were waited for; matrix products, arithmetic and copies ran while one was open for 37% of the time, Pallas kernels for 0%

commit v1 on v0

v1 whole, which is shorter than its diff:
```python
import functools
import math

import jax
import jax.numpy as jnp
from jax import lax
from jax.experimental import pallas as pl
from jax.experimental.pallas import tpu as pltpu
from jax.sharding import PartitionSpec as P

HEAD = 128
MASKED = -1e30
CHUNKS = 4
MESH = pl.DeviceIdType.MESH


def body(
    n_ctx, nblk,
    q_ref, k_ref, v_ref, pick_near, pick_far, bias_ref, out_ref,
    near, forwarded, big, inner, outer, far, far_pack, relay_pack, got_near, got_far,
    acc, top, tot,
    s_list, s_near, s_full, s_far, s_relay, s_fwd, s_pack,
    r_list, r_near, r_big, r_far, r_fwd, r_outer,
):
    rows, width = q_ref.shape
    heads = width // HEAD
    bs = rows // nblk
    half = rows // 2
    cap1, cap2, cap3 = nblk // 2, nblk // 4, nblk // 8
    rate = math.log2(math.e) / math.sqrt(HEAD)

    d = lax.axis_index("ctx")
    place = lax.rem(d, 4)
    quad = d // 4
    quads = n_ctx // 4
    left = place < 2
    s = jnp.where(left, 1, -1)
    gate = (place == 1) | (place == 2)
    outermost = jnp.logical_not(gate)
    has_out = jnp.where(left, quad > 0, quad < quads - 1)
    has_in = jnp.where(left, quad < quads - 1, quad > 0)
    side_in = jnp.where(left, 1, 0)
    side_out = 1 - side_in
    twin = jnp.where(gate, d - s, d + s)
    relay_to = d + 3 * s
    relay_from = d - 3 * s
    relays = gate & has_in
    gets_relay = outermost & has_out
    forwards = gate | has_out
    fwd_arrives = outermost | has_out
    full_to = jnp.where(gate, d + s, d + 2 * s)
    full_slot = jnp.where(gate, 0, 1)

    fars = []
    for distance in (4, 8):
        fars.append((d + distance, d + distance < n_ctx))
        fars.append((d - distance, d - distance >= 0))

    def to(device):
        return {"ctx": device}

    barrier = pltpu.get_barrier_semaphore()
    partners = [(p, ok) for p, ok in fars]
    always = jnp.bool_(True)
    partners += [
        (twin, always),
        (d + 2 * s, always),
        (d + s, gate),
        (relay_to, relays),
        (relay_from, gets_relay),
    ]
    count = jnp.int32(0)
    for p, ok in partners:
        count = count + ok.astype(jnp.int32)

        @pl.when(ok)
        def _(p=p):
            pl.semaphore_signal(barrier, inc=1, device_id=to(p), device_id_type=MESH)

    pl.semaphore_wait(barrier, count)

    def remote(src, dst, ssem, rsem, device):
        return pltpu.make_async_remote_copy(
            src_ref=src, dst_ref=dst, send_sem=ssem, recv_sem=rsem,
            device_id=to(device), device_id_type=MESH,
        )

    far_rows = (cap2 * bs, cap2 * bs, cap3 * bs, cap3 * bs)
    far_start = (0, cap2 * bs, 2 * cap2 * bs, (2 * cap2 + cap3) * bs)

    def pick_copy(i, device):
        if i == 4:
            return remote(pick_near.at[side_out], got_near, s_list.at[4], r_list.at[4], device)
        r = pl.ds(far_start[i], far_rows[i])
        return remote(pick_far.at[r], got_far.at[r], s_list.at[i], r_list.at[i], device)

    flip = (1, 0, 3, 2)
    sends_list = [(flip[i], p, ok) for i, (p, ok) in enumerate(fars)] + [(4, relay_from, gets_relay)]
    has_list = [(i, p, ok) for i, (p, ok) in enumerate(fars)] + [(4, relay_to, relays)]

    step_cols = 4 * HEAD if width % (4 * HEAD) == 0 else HEAD

    def gather(pick, sources, dst_of):
        def go(i, carry):
            cols = pl.ds(pl.multiple_of(i * step_cols, step_cols), step_cols)
            for kv in range(2):
                rows_got = jnp.dot(pick, sources[kv](cols), preferred_element_type=jnp.float32)
                dst_of(kv, cols, rows_got.astype(jnp.bfloat16))
            return carry

        lax.fori_loop(0, width // step_cols, go, 0)

    def near_copy(c):
        return remote((k_ref, v_ref)[c], near.at[c], s_near.at[c], r_near.at[c], twin)

    def part(c):
        return c // 2, pl.ds((c % 2) * half, half)

    def full_copy(c):
        kv, r = part(c)
        return remote(
            (k_ref, v_ref)[kv].at[r], big.at[full_slot, kv, r],
            s_full.at[c], r_big.at[full_slot, c], full_to,
        )

    def relay_copy(c):
        kv, r = part(c)
        return remote(big.at[1, kv, r], big.at[0, kv, r], s_relay.at[c], r_big.at[0, c], relay_to)

    def fwd_copy(c):
        kv, r = part(c)
        return remote(big.at[0, kv, r], forwarded.at[kv, r], s_fwd.at[c], r_fwd.at[c], twin)

    def big_wait(slot, c):
        kv, r = part(c)
        remote(big.at[slot, kv, r], big.at[slot, kv, r], s_relay.at[c], r_big.at[slot, c], twin).wait_recv()

    def far_copy(i):
        r = pl.ds(far_start[i], far_rows[i])
        return remote(far_pack.at[:, r], far.at[:, r], s_far.at[i], r_far.at[i], fars[i][0])

    def pack_copy():
        return remote(relay_pack, outer, s_pack, r_outer, relay_to)

    for slot, p, ok in sends_list:
        @pl.when(ok)
        def _(slot=slot, p=p):
            pick_copy(slot, p).start()

    for c in range(CHUNKS):
        full_copy(c).start()
    for c in range(2):
        near_copy(c).start()

    for slot, p, ok in has_list:
        @pl.when(ok)
        def _(slot=slot, p=p):
            pick_copy(slot, p).wait_recv()
            if slot < 4:
                r = pl.ds(far_start[slot], far_rows[slot])

                def put(kv, cols, x):
                    far_pack[kv, r, cols] = x

                gather(got_far[r, :], (lambda c: k_ref[:, c], lambda c: v_ref[:, c]), put)
                far_copy(slot).start()

    def full_bias(side):
        return bias_ref[side]

    def listed_bias(side):
        return bias_ref[2 + side, :, pl.ds(0, cap1 * bs)]

    def wide(x, n):
        k = n // HEAD
        whole = jnp.concatenate([x] * k, axis=1) if k > 1 else x
        if n % HEAD:
            whole = jnp.concatenate([x] * (k + 1), axis=1)[:, :n]
        return whole

    def folded(p):
        n = p.shape[1]
        total = p[:, :HEAD]
        for i in range(1, n // HEAD):
            total = total + p[:, i * HEAD:(i + 1) * HEAD]
        return total

    def attend(keys, values, bias, first=False):
        def one(h):
            cols = pl.ds(pl.multiple_of(h * HEAD, HEAD), HEAD)
            sc = lax.dot_general(
                q_ref[:, cols], keys(cols), (((1,), (1,)), ((), ())),
                preferred_element_type=jnp.float32,
            ) * rate
            if bias is not None:
                sc = sc + bias
            n = sc.shape[1]
            best = jnp.broadcast_to(jnp.max(sc, axis=1, keepdims=True), (rows, HEAD))
            if not first:
                old = top[h]
                best = jnp.maximum(old, best)
            p = jnp.exp2(sc - wide(best, n))
            mixed = jnp.dot(
                p.astype(jnp.bfloat16), values(cols), preferred_element_type=jnp.float32
            )
            part_sum = folded(p)
            if first:
                tot[h] = part_sum
                acc[h] = mixed
            else:
                factor = jnp.exp2(old - best)
                tot[h] = tot[h] * factor + part_sum
                acc[h] = acc[h] * factor + mixed
            top[h] = best

        def step(i, carry):
            one(2 * i)
            one(2 * i + 1)
            return carry

        if heads % 2:
            lax.fori_loop(0, heads, lambda i, c: (one(i), c)[1], 0)
        else:
            lax.fori_loop(0, heads // 2, step, 0)

    def put_inner(kv, cols, x):
        inner[kv, :, cols] = x

    def put_outer(kv, cols, x):
        outer[kv, :, cols] = x

    attend(lambda c: k_ref[:, c], lambda c: v_ref[:, c], None, first=True)

    for c in range(2):
        near_copy(c).wait_recv()
    attend(
        lambda c: near[0, :, c], lambda c: near[1, :, c],
        full_bias(jnp.where(gate, side_out, side_in)),
    )

    @pl.when(gate)
    def _():
        for c in range(2):
            big_wait(1, c)

            @pl.when(has_in)
            def _(c=c):
                relay_copy(c).start()

            big_wait(0, c)
            fwd_copy(c).start()

    arrives = [fars[1], fars[0], fars[3], fars[2]]
    for i in range(4):
        @pl.when(arrives[i][1])
        def _(i=i):
            far_copy(i).wait_recv()

        @pl.when(jnp.logical_not(arrives[i][1]))
        def _(i=i):
            for kv in range(2):
                far[kv, pl.ds(far_start[i], far_rows[i]), :] = jnp.zeros(
                    (far_rows[i], width), far.dtype
                )

    spare = (-sum(far_rows)) % HEAD
    if spare:
        for kv in range(2):
            far[kv, pl.ds(sum(far_rows), spare), :] = jnp.zeros((spare, width), far.dtype)
    far_bias = bias_ref[4, :, pl.ds(0, sum(far_rows) + spare)]
    attend(lambda c: far[0, :, c], lambda c: far[1, :, c], far_bias)

    @pl.when(gate)
    def _():
        for c in range(2, CHUNKS):
            big_wait(1, c)

            @pl.when(has_in)
            def _(c=c):
                relay_copy(c).start()

            big_wait(0, c)
            fwd_copy(c).start()

        @pl.when(has_in)
        def _():
            def put_relay(kv, cols, x):
                relay_pack[kv, :, cols] = x

            gather(got_near[...], (lambda c: big[0, 0, :, c], lambda c: big[0, 1, :, c]), put_relay)
            pack_copy().start()

        gather(pick_near[side_in], (lambda c: big[1, 0, :, c], lambda c: big[1, 1, :, c]), put_inner)

    @pl.when(gets_relay)
    def _():
        for c in range(CHUNKS):
            big_wait(0, c)
            fwd_copy(c).start()

    @pl.when(outermost)
    def _():
        for c in range(CHUNKS):
            fwd_copy(c).wait_recv()
        gather(pick_near[side_in], (lambda c: forwarded[0, :, c], lambda c: forwarded[1, :, c]), put_inner)

    attend(lambda c: inner[0, :, c], lambda c: inner[1, :, c], listed_bias(side_in))

    @pl.when(forwards)
    def _():
        attend(
            lambda c: big[0, 0, :, c], lambda c: big[0, 1, :, c],
            full_bias(jnp.where(gate, side_in, side_out)),
        )

    @pl.when(gate & has_out)
    def _():
        for c in range(CHUNKS):
            fwd_copy(c).wait_recv()
        gather(pick_near[side_out], (lambda c: forwarded[0, :, c], lambda c: forwarded[1, :, c]), put_outer)

    @pl.when(gets_relay)
    def _():
        pack_copy().wait_recv()

    @pl.when(has_out)
    def _():
        attend(lambda c: outer[0, :, c], lambda c: outer[1, :, c], listed_bias(side_out))

    def finish(h, carry):
        cols = pl.ds(pl.multiple_of(h * HEAD, HEAD), HEAD)
        total = jnp.sum(tot[h], axis=1, keepdims=True)
        out_ref[:, cols] = (acc[h] / total).astype(out_ref.dtype)
        return carry

    lax.fori_loop(0, heads, finish, 0)

    for slot, p, ok in sends_list:
        @pl.when(ok)
        def _(slot=slot, p=p):
            pick_copy(slot, p).wait_send()
    for c in range(CHUNKS):
        full_copy(c).wait_send()
    for c in range(2):
        near_copy(c).wait_send()
    for i, (p, ok) in enumerate(fars):
        @pl.when(ok)
        def _(i=i):
            far_copy(i).wait_send()

    @pl.when(relays)
    def _():
        for c in range(CHUNKS):
            relay_copy(c).wait_send()
        pack_copy().wait_send()

    @pl.when(forwards)
    def _():
        for c in range(CHUNKS):
            fwd_copy(c).wait_send()


def shards(n_ctx, queries, keys, values, kv_lists, kv_counts):
    rows, width = queries.shape
    heads = width // HEAD
    nblk = kv_lists.shape[3]
    levels = kv_lists.shape[1]
    bs = rows // nblk
    counts = kv_counts[0]
    block = jnp.arange(rows, dtype=jnp.int32) // bs
    slot = jnp.arange(nblk, dtype=jnp.int32)
    named = kv_lists[0, 0][:, :, None] == block[None, None, :]
    used = slot[None, :, None] < counts[0][:, None, None]
    full = jnp.any(named & used, axis=1)
    listed = block[None, :] < counts[1][:, None]
    start, far_seen = 0, jnp.zeros((rows,), jnp.bool_)
    for level in (2, 3):
        for side in range(2):
            at = block - start
            far_seen = far_seen | ((at >= 0) & (at < counts[level, side]))
            start += nblk >> level
    seen = jnp.concatenate([full, listed, far_seen[None], jnp.zeros((3, rows), jnp.bool_)], axis=0)
    row = jnp.arange(rows, dtype=jnp.int32)

    def picks(level):
        cap = nblk >> level
        wanted = kv_lists[0, level, :, :cap, None] * bs + jnp.arange(bs, dtype=jnp.int32)
        wanted = wanted.reshape(2, cap * bs, 1)
        return (wanted == row).astype(jnp.bfloat16)

    pick_near = picks(1)
    pick_far = jnp.concatenate([picks(2).reshape(-1, rows), picks(3).reshape(-1, rows)], axis=0)
    bias = jnp.where(seen, 0.0, MASKED).astype(jnp.float32)[:, None, :]
    cap1 = nblk // 2
    far_rows = 2 * (nblk // 4 + nblk // 8) * bs
    far_room = far_rows + (-far_rows) % HEAD
    kv = jnp.bfloat16
    vmem = pl.BlockSpec(memory_space=pltpu.VMEM)
    dma = pltpu.SemaphoreType.DMA
    return pl.pallas_call(
        functools.partial(body, n_ctx, nblk),
        out_shape=jax.ShapeDtypeStruct((rows, width), jnp.bfloat16),
        in_specs=[vmem] * 6,
        out_specs=vmem,
        scratch_shapes=[
            pltpu.VMEM((2, rows, width), kv),
            pltpu.VMEM((2, rows, width), kv),
            pltpu.VMEM((2, 2, rows, width), kv),
            pltpu.VMEM((2, cap1 * bs, width), kv),
            pltpu.VMEM((2, cap1 * bs, width), kv),
            pltpu.VMEM((2, far_room, width), kv),
            pltpu.VMEM((2, far_rows, width), kv),
            pltpu.VMEM((2, cap1 * bs, width), kv),
            pltpu.VMEM((cap1 * bs, rows), kv),
            pltpu.VMEM((far_rows, rows), kv),
            pltpu.VMEM((heads, rows, HEAD), jnp.float32),
            pltpu.VMEM((heads, rows, HEAD), jnp.float32),
            pltpu.VMEM((heads, rows, HEAD), jnp.float32),
            dma((5,)), dma((2,)), dma((CHUNKS,)), dma((4,)), dma((CHUNKS,)), dma((CHUNKS,)), dma,
            dma((5,)), dma((2,)), dma((2, CHUNKS)), dma((4,)), dma((CHUNKS,)), dma,
        ],
        compiler_params=pltpu.CompilerParams(
            collective_id=0, has_side_effects=True, vmem_limit_bytes=60 * 1024 * 1024
        ),
        name="radial",
    )(queries, keys, values, pick_near, pick_far, bias)


def solution(mesh):
    in_specs = (
        P(("groups", "ctx"), None),
        P(("groups", "ctx"), None),
        P(("groups", "ctx"), None),
        P("ctx", None, None, None),
        P("ctx", None, None),
    )
    out_specs = P(("groups", "ctx"), None)
    return jax.shard_map(
        functools.partial(shards, mesh.shape["ctx"]),
        mesh=mesh, in_specs=in_specs, out_specs=out_specs, check_vma=False,
    )
```

time: 221 us -> 111 us (0.50)
  the two profiles are of different devices: /device:TPU:10 before, /device:TPU:5 now
where the time goes in v1:
time: 111 us; the launch traced here: 110 us
  Pallas kernels  96.6 us (87%)
  other arithmetic  7.2 us (6%)
  local copies, waits for them, and re-layouts  6.41 us (6%)
    pallas_call x1, Pallas kernels, shards(): pl.pallas_call(functools.partial(body, n_ctx, nblk), out_shape=jax.ShapeD...  96.6 us
    concatenate x3, other arithmetic, shards(): jnp.concatenate([full, listed, far_seen[None], jnp.zeros((3, rows), jnp.b...  2.69 us
    unnamed x1, local copies, waits for them, and re-layouts  2.46 us

profile of v1, /device:TPU:5, one launch (start us, length us, event | category | flops | bytes accessed | tf_op | source)
XLA Modules:
  0.0 110.3 jit_solution(13285015124206005841)
XLA Ops:
  0.0 0.8 multiply_reduce_fusion
  0.8 0.1 add.147
  0.9 0.1 add.148
  1.0 0.1 pad.3.clone
  1.0 0.7 multiply_bitcast_fusion
  1.7 0.1 add.140
  1.8 0.1 add.141
  1.9 0.7 multiply_bitcast_fusion.1
  2.6 0.7 slice_bitcast_fusion
  3.3 0.1 add.143
  3.3 0.1 add.145
  3.4 1.0 slice_reduce_fusion.1
  4.4 0.1 iota_compare_fusion.3
  4.5 0.1 and_reduce_fusion
  4.6 0.1 compare_bitcast_fusion
  4.6 0.1 add.137
  4.7 1.5 %fusion.1 = (s32[1,1]{0,1:T(1,128)}, s32[1,1]{0,1:T(1,128)}, s32[1,1]{0,1:T(1,128)}, s32[1,1]{0,1:T(1,128)}) fusion(s32[4,2]{0,1:T(2,128)} %bitcast.18), kind=kLoop, calls=%fused_computation.26 | loop fusion | bytes 32 | tf_op jit(solution)/shard_map/slice | solution.py:380
  6.2 2.5 %or_bitcast_fusion = pred[1,1,256]{2,0,1:T(4,128)(4,1)S(1)} fusion(s32[]{:T(128)} %bitcast.9, s32[]{:T(128)} %bitcast.8, s32[]{:T(128)} %bitcast.7, s32[]{:T(128)} %bitcast.6), kind=kLoop, calls=%fused_computation.8 | loop fusion | flops 6656 | bytes 272 | tf_op jit(solution)/shard_map/concatenate | solution.py:382
  8.8 0.1 add_add_fusion
  8.9 0.1 add.134
  8.9 0.1 add.135
  9.0 0.6 copy_select_fusion.bias_ref
  9.6 0.1 iota_compare_fusion.2
  9.7 0.1 iota_compare_fusion.1
  9.8 0.6 add_convert_fusion.pick_far
  10.4 0.8 fusion.pick_near
  11.2 96.6 %radial.1 = bf16[256,2560]{1,0:T(8,128)(2,1)} custom-call(bf16[256,2560]{1,0:T(8,128)(2,1)} %q_ref.1, bf16[256,2560]{1,0:T(8,128)(2,1)} %k_ref.1, bf16[256,2560]{1,0:T(8,128)(2,1)} %v_ref.1, bf16[2,128,256]{2,1,0:T(8,128)(2,1)} %fusion.pick_near, bf16[192,256]{1,0:T(8,128)(2,1)} %add_convert_fusion.pick_far, f32[8,1,256]{2,1,0:T(1,128)} %copy_select_fusion.bias_ref), custom_call_target="tpu_custom_call" | custom-call | tf_op jit(solution)/shard_map/radial/pallas_call | solution.py:400
  107.8 2.5 %copy.12 = bf16[256,2560]{1,0:T(8,128)(2,1)} copy(bf16[256,2560]{1,0:T(8,128)(2,1)} %radial.1) | data formatting | bytes 2621440
  (8 shorter events, 0.0 us)

commit v2 on v1

--- a/solution.py
+++ b/solution.py
@@ -16,11 +16,11 @@
 
 def body(
     n_ctx, nblk,
-    q_ref, k_ref, v_ref, pick_near, pick_far, bias_ref, out_ref,
-    near, forwarded, big, inner, outer, far, far_pack, relay_pack, got_near, got_far,
+    q_ref, k_ref, v_ref, lists, counts, out_ref,
+    near, forwarded, big, inner, outer, far, far_pack, relay_pack, hop, pick_near, pick_far, got_near, got_far,
     acc, top, tot,
-    s_list, s_near, s_full, s_far, s_relay, s_fwd, s_pack,
-    r_list, r_near, r_big, r_far, r_fwd, r_outer,
+    s_list, s_near, s_full, s_far, s_relay, s_fwd, s_pack, s_hop,
+    r_list, r_near, r_big, r_far, r_fwd, r_outer, r_hop,
 ):
     rows, width = q_ref.shape
     heads = width // HEAD
@@ -48,13 +48,28 @@
     gets_relay = outermost & has_out
     forwards = gate | has_out
     fwd_arrives = outermost | has_out
-    full_to = jnp.where(gate, d + s, d + 2 * s)
-    full_slot = jnp.where(gate, 0, 1)
 
     fars = []
     for distance in (4, 8):
         fars.append((d + distance, d + distance < n_ctx))
         fars.append((d - distance, d - distance >= 0))
+
+    far_rows = (cap2 * bs, cap2 * bs, cap3 * bs, cap3 * bs)
+    far_start = (0, cap2 * bs, 2 * cap2 * bs, (2 * cap2 + cap3) * bs)
+    ahead = lax.broadcasted_iota(jnp.int32, (bs, rows), 1) - lax.broadcasted_iota(
+        jnp.int32, (bs, rows), 0
+    )
+
+    def single_ones(level, side, j):
+        hit = ahead == lists[0, level, side, j] * bs
+        return jnp.where(hit, 1.0, 0.0).astype(jnp.bfloat16)
+
+    for i in range(4):
+        for j in range(far_rows[i] // bs):
+            pick_far[pl.ds(far_start[i] + j * bs, bs), :] = single_ones(2 + i // 2, i % 2, j)
+    for side in range(2):
+        for j in range(cap1):
+            pick_near[side, pl.ds(j * bs, bs), :] = single_ones(1, side, j)
 
     def to(device):
         return {"ctx": device}
@@ -64,8 +79,8 @@
     always = jnp.bool_(True)
     partners += [
         (twin, always),
-        (d + 2 * s, always),
         (d + s, gate),
+        (d + 3 * s, outermost),
         (relay_to, relays),
         (relay_from, gets_relay),
     ]
@@ -85,9 +100,6 @@
             device_id=to(device), device_id_type=MESH,
         )
 
-    far_rows = (cap2 * bs, cap2 * bs, cap3 * bs, cap3 * bs)
-    far_start = (0, cap2 * bs, 2 * cap2 * bs, (2 * cap2 + cap3) * bs)
-
     def pick_copy(i, device):
         if i == 4:
             return remote(pick_near.at[side_out], got_near, s_list.at[4], r_list.at[4], device)
@@ -103,25 +115,29 @@
     def gather(pick, sources, dst_of):
         def go(i, carry):
             cols = pl.ds(pl.multiple_of(i * step_cols, step_cols), step_cols)
-            for kv in range(2):
+            for kv in range(len(sources)):
                 rows_got = jnp.dot(pick, sources[kv](cols), preferred_element_type=jnp.float32)
                 dst_of(kv, cols, rows_got.astype(jnp.bfloat16))
             return carry
 
         lax.fori_loop(0, width // step_cols, go, 0)
 
-    def near_copy(c):
-        return remote((k_ref, v_ref)[c], near.at[c], s_near.at[c], r_near.at[c], twin)
-
     def part(c):
         return c // 2, pl.ds((c % 2) * half, half)
 
-    def full_copy(c):
+    def near_copy(c):
+        kv, r = part(c)
+        return remote((k_ref, v_ref)[kv].at[r], near.at[kv, r], s_near.at[c], r_near.at[c], twin)
+
+    def cross_copy(c):
         kv, r = part(c)
         return remote(
-            (k_ref, v_ref)[kv].at[r], big.at[full_slot, kv, r],
-            s_full.at[c], r_big.at[full_slot, c], full_to,
+            (k_ref, v_ref)[kv].at[r], big.at[0, kv, r], s_full.at[0, c], r_big.at[0, c], d + s
         )
+
+    def twin_copy(c):
+        kv, r = part(c)
+        return remote(near.at[kv, r], big.at[1, kv, r], s_full.at[1, c], r_big.at[1, c], d + s)
 
     def relay_copy(c):
         kv, r = part(c)
@@ -139,8 +155,16 @@
         r = pl.ds(far_start[i], far_rows[i])
         return remote(far_pack.at[:, r], far.at[:, r], s_far.at[i], r_far.at[i], fars[i][0])
 
-    def pack_copy():
-        return remote(relay_pack, outer, s_pack, r_outer, relay_to)
+    def pack_copy(kv):
+        return remote(relay_pack.at[kv], outer.at[kv], s_pack.at[kv], r_outer.at[kv], relay_to)
+
+    def hop_copy():
+        kv, r = part(CHUNKS - 1)
+        return remote((k_ref, v_ref)[kv].at[r], hop, s_hop.at[0], r_hop, d - 4 * s)
+
+    def hop_on_copy():
+        kv, r = part(CHUNKS - 1)
+        return remote(hop, big.at[0, kv, r], s_hop.at[1], r_big.at[0, CHUNKS - 1], d + 3 * s)
 
     for slot, p, ok in sends_list:
         @pl.when(ok)
@@ -148,9 +172,15 @@
             pick_copy(slot, p).start()
 
     for c in range(CHUNKS):
-        full_copy(c).start()
-    for c in range(2):
         near_copy(c).start()
+
+    @pl.when(gate)
+    def _():
+        cross_copy(0).start()
+
+    @pl.when(gets_relay)
+    def _():
+        hop_copy().start()
 
     for slot, p, ok in has_list:
         @pl.when(ok)
@@ -165,11 +195,32 @@
                 gather(got_far[r, :], (lambda c: k_ref[:, c], lambda c: v_ref[:, c]), put)
                 far_copy(slot).start()
 
+    @pl.when(gate)
+    def _():
+        for c in range(CHUNKS):
+            near_copy(c).wait_recv()
+        twin_copy(0).start()
+        cross_copy(1).start()
+        twin_copy(1).start()
+        cross_copy(2).start()
+        cross_copy(3).start()
+        twin_copy(2).start()
+        twin_copy(3).start()
+
+    def as_bias(seen):
+        return jnp.where(seen, 0.0, MASKED).astype(jnp.float32)
+
     def full_bias(side):
-        return bias_ref[side]
+        block = lax.broadcasted_iota(jnp.int32, (1, rows), 1) // bs
+        seen = jnp.zeros((1, rows), jnp.int32)
+        for j in range(nblk):
+            hit = (block == lists[0, 0, side, j]) & (jnp.full((1, rows), j) < counts[0, 0, side])
+            seen = seen + hit.astype(jnp.int32)
+        return as_bias(seen > 0)
 
     def listed_bias(side):
-        return bias_ref[2 + side, :, pl.ds(0, cap1 * bs)]
+        column = lax.broadcasted_iota(jnp.int32, (1, cap1 * bs), 1)
+        return as_bias(column < counts[0, 1, side] * bs)
 
     def wide(x, n):
         k = n // HEAD
@@ -231,24 +282,48 @@
 
     attend(lambda c: k_ref[:, c], lambda c: v_ref[:, c], None, first=True)
 
-    for c in range(2):
-        near_copy(c).wait_recv()
+    @pl.when(outermost & has_in)
+    def _():
+        hop_copy().wait_recv()
+        hop_on_copy().start()
+
+    @pl.when(outermost)
+    def _():
+        for c in range(CHUNKS):
+            near_copy(c).wait_recv()
+
     attend(
         lambda c: near[0, :, c], lambda c: near[1, :, c],
         full_bias(jnp.where(gate, side_out, side_in)),
     )
 
+    def pass_cross(c):
+        big_wait(0, c)
+        fwd_copy(c).start()
+
+    def pass_twin(c):
+        big_wait(1, c)
+
+        @pl.when(has_in)
+        def _():
+            relay_copy(c).start()
+
+    def pass_listed(kv):
+        @pl.when(has_in)
+        def _():
+            def put_relay(_, cols, x):
+                relay_pack[kv, :, cols] = x
+
+            gather(got_near[...], (lambda c: big[0, kv, :, c],), put_relay)
+            pack_copy(kv).start()
+
     @pl.when(gate)
     def _():
-        for c in range(2):
-            big_wait(1, c)
-
-            @pl.when(has_in)
-            def _(c=c):
-                relay_copy(c).start()
-
-            big_wait(0, c)
-            fwd_copy(c).start()
+        pass_twin(0)
+        pass_cross(0)
+        pass_cross(1)
+        pass_listed(0)
+        pass_twin(1)
 
     arrives = [fars[1], fars[0], fars[3], fars[2]]
     for i in range(4):
@@ -267,65 +342,70 @@
     if spare:
         for kv in range(2):
             far[kv, pl.ds(sum(far_rows), spare), :] = jnp.zeros((spare, width), far.dtype)
-    far_bias = bias_ref[4, :, pl.ds(0, sum(far_rows) + spare)]
+    column = lax.broadcasted_iota(jnp.int32, (1, sum(far_rows) + spare), 1)
+    limit = jnp.zeros(column.shape, jnp.int32)
+    for i in range(4):
+        end = far_start[i] + counts[0, 2 + i // 2, i % 2] * bs
+        limit = jnp.where(column >= far_start[i], end, limit)
+    limit = jnp.where(column >= sum(far_rows), 0, limit)
+    far_bias = as_bias(column < limit)
     attend(lambda c: far[0, :, c], lambda c: far[1, :, c], far_bias)
 
-    @pl.when(gate)
-    def _():
-        for c in range(2, CHUNKS):
-            big_wait(1, c)
-
-            @pl.when(has_in)
-            def _(c=c):
-                relay_copy(c).start()
-
-            big_wait(0, c)
-            fwd_copy(c).start()
-
-        @pl.when(has_in)
-        def _():
-            def put_relay(kv, cols, x):
-                relay_pack[kv, :, cols] = x
-
-            gather(got_near[...], (lambda c: big[0, 0, :, c], lambda c: big[0, 1, :, c]), put_relay)
-            pack_copy().start()
-
-        gather(pick_near[side_in], (lambda c: big[1, 0, :, c], lambda c: big[1, 1, :, c]), put_inner)
-
-    @pl.when(gets_relay)
-    def _():
-        for c in range(CHUNKS):
-            big_wait(0, c)
-            fwd_copy(c).start()
-
-    @pl.when(outermost)
-    def _():
-        for c in range(CHUNKS):
-            fwd_copy(c).wait_recv()
-        gather(pick_near[side_in], (lambda c: forwarded[0, :, c], lambda c: forwarded[1, :, c]), put_inner)
-
-    attend(lambda c: inner[0, :, c], lambda c: inner[1, :, c], listed_bias(side_in))
-
-    @pl.when(forwards)
-    def _():
+    def attend_inner():
+        attend(lambda c: inner[0, :, c], lambda c: inner[1, :, c], listed_bias(side_in))
+
+    def attend_big():
         attend(
             lambda c: big[0, 0, :, c], lambda c: big[0, 1, :, c],
             full_bias(jnp.where(gate, side_in, side_out)),
         )
 
-    @pl.when(gate & has_out)
-    def _():
+    def attend_outer():
+        attend(lambda c: outer[0, :, c], lambda c: outer[1, :, c], listed_bias(side_out))
+
+    @pl.when(gate)
+    def _():
+        pass_cross(2)
+        pass_cross(3)
+        pass_listed(1)
+        attend_big()
+        pass_twin(2)
+        big_wait(1, 3)
+        gather(pick_near[side_in], (lambda c: big[1, 0, :, c], lambda c: big[1, 1, :, c]), put_inner)
+        attend_inner()
+
+        @pl.when(has_out)
+        def _():
+            for c in range(CHUNKS):
+                fwd_copy(c).wait_recv()
+            gather(
+                pick_near[side_out],
+                (lambda c: forwarded[0, :, c], lambda c: forwarded[1, :, c]), put_outer,
+            )
+            attend_outer()
+
+    @pl.when(outermost)
+    def _():
+        @pl.when(has_out)
+        def _():
+            for c in (0, 1, 3):
+                pass_cross(c)
+
         for c in range(CHUNKS):
             fwd_copy(c).wait_recv()
-        gather(pick_near[side_out], (lambda c: forwarded[0, :, c], lambda c: forwarded[1, :, c]), put_outer)
-
-    @pl.when(gets_relay)
-    def _():
-        pack_copy().wait_recv()
-
-    @pl.when(has_out)
-    def _():
-        attend(lambda c: outer[0, :, c], lambda c: outer[1, :, c], listed_bias(side_out))
+        gather(
+            pick_near[side_in],
+            (lambda c: forwarded[0, :, c], lambda c: forwarded[1, :, c]), put_inner,
+        )
+        attend_inner()
+
+        @pl.when(has_out)
+        def _():
+            pass_cross(2)
+            for kv in range(2):
+                pack_copy(kv).wait_recv()
+            attend_outer()
+            attend_big()
 
     def finish(h, carry):
         cols = pl.ds(pl.multiple_of(h * HEAD, HEAD), HEAD)
@@ -340,9 +420,14 @@
         def _(slot=slot, p=p):
             pick_copy(slot, p).wait_send()
     for c in range(CHUNKS):
-        full_copy(c).wait_send()
-    for c in range(2):
         near_copy(c).wait_send()
+
+    @pl.when(gate)
+    def _():
+        for c in range(CHUNKS):
+            cross_copy(c).wait_send()
+            twin_copy(c).wait_send()
+
     for i, (p, ok) in enumerate(fars):
         @pl.when(ok)
         def _(i=i):
@@ -350,9 +435,18 @@
 
     @pl.when(relays)
     def _():
-        for c in range(CHUNKS):
+        for c in range(CHUNKS - 1):
             relay_copy(c).wait_send()
-        pack_copy().wait_send()
+        for kv in range(2):
+            pack_copy(kv).wait_send()
+
+    @pl.when(gets_relay)
+    def _():
+        hop_copy().wait_send()
+
+    @pl.when(outermost & has_in)
+    def _():
+        hop_on_copy().wait_send()
 
     @pl.when(forwards)
     def _():
@@ -364,43 +458,18 @@
     rows, width = queries.shape
     heads = width // HEAD
     nblk = kv_lists.shape[3]
-    levels = kv_lists.shape[1]
     bs = rows // nblk
-    counts = kv_counts[0]
-    block = jnp.arange(rows, dtype=jnp.int32) // bs
-    slot = jnp.arange(nblk, dtype=jnp.int32)
-    named = kv_lists[0, 0][:, :, None] == block[None, None, :]
-    used = slot[None, :, None] < counts[0][:, None, None]
-    full = jnp.any(named & used, axis=1)
-    listed = block[None, :] < counts[1][:, None]
-    start, far_seen = 0, jnp.zeros((rows,), jnp.bool_)
-    for level in (2, 3):
-        for side in range(2):
-            at = block - start
-            far_seen = far_seen | ((at >= 0) & (at < counts[level, side]))
-            start += nblk >> level
-    seen = jnp.concatenate([full, listed, far_seen[None], jnp.zeros((3, rows), jnp.bool_)], axis=0)
-    row = jnp.arange(rows, dtype=jnp.int32)
-
-    def picks(level):
-        cap = nblk >> level
-        wanted = kv_lists[0, level, :, :cap, None] * bs + jnp.arange(bs, dtype=jnp.int32)
-        wanted = wanted.reshape(2, cap * bs, 1)
-        return (wanted == row).astype(jnp.bfloat16)
-
-    pick_near = picks(1)
-    pick_far = jnp.concatenate([picks(2).reshape(-1, rows), picks(3).reshape(-1, rows)], axis=0)
-    bias = jnp.where(seen, 0.0, MASKED).astype(jnp.float32)[:, None, :]
     cap1 = nblk // 2
     far_rows = 2 * (nblk // 4 + nblk // 8) * bs
     far_room = far_rows + (-far_rows) % HEAD
     kv = jnp.bfloat16
     vmem = pl.BlockSpec(memory_space=pltpu.VMEM)
+    smem = pl.BlockSpec(memory_space=pltpu.SMEM)
     dma = pltpu.SemaphoreType.DMA
     return pl.pallas_call(
         functools.partial(body, n_ctx, nblk),
         out_shape=jax.ShapeDtypeStruct((rows, width), jnp.bfloat16),
-        in_specs=[vmem] * 6,
+        in_specs=[vmem, vmem, vmem, smem, smem],
         out_specs=vmem,
         scratch_shapes=[
             pltpu.VMEM((2, rows, width), kv),
@@ -411,19 +480,22 @@
             pltpu.VMEM((2, far_room, width), kv),
             pltpu.VMEM((2, far_rows, width), kv),
             pltpu.VMEM((2, cap1 * bs, width), kv),
+            pltpu.VMEM((rows // 2, width), kv),
+            pltpu.VMEM((2, cap1 * bs, rows), kv),
+            pltpu.VMEM((far_rows, rows), kv),
             pltpu.VMEM((cap1 * bs, rows), kv),
             pltpu.VMEM((far_rows, rows), kv),
             pltpu.VMEM((heads, rows, HEAD), jnp.float32),
             pltpu.VMEM((heads, rows, HEAD), jnp.float32),
             pltpu.VMEM((heads, rows, HEAD), jnp.float32),
-            dma((5,)), dma((2,)), dma((CHUNKS,)), dma((4,)), dma((CHUNKS,)), dma((CHUNKS,)), dma,
-            dma((5,)), dma((2,)), dma((2, CHUNKS)), dma((4,)), dma((CHUNKS,)), dma,
+            dma((5,)), dma((CHUNKS,)), dma((2, CHUNKS)), dma((4,)), dma((CHUNKS,)), dma((CHUNKS,)), dma((2,)), dma((2,)),
+            dma((5,)), dma((CHUNKS,)), dma((2, CHUNKS)), dma((4,)), dma((CHUNKS,)), dma((2,)), dma,
         ],
         compiler_params=pltpu.CompilerParams(
             collective_id=0, has_side_effects=True, vmem_limit_bytes=60 * 1024 * 1024
         ),
         name="radial",
-    )(queries, keys, values, pick_near, pick_far, bias)
+    )(queries, keys, values, kv_lists, kv_counts)
 
 
 def solution(mesh):

time: 111 us -> 94.7 us (0.85)
  the two profiles are of different devices: /device:TPU:5 before, /device:TPU:17 now
where the time goes in v2:
time: 94.7 us; the launch traced here: 93.1 us
  Pallas kernels  89.3 us (94%)
  local copies, waits for them, and re-layouts  3.79 us (4%)
    pallas_call x1, Pallas kernels, shards(): pl.pallas_call(functools.partial(body, n_ctx, nblk), out_shape=jax.ShapeD...  89.3 us
    unnamed x2, local copies, waits for them, and re-layouts  3.79 us

profile of v2, /device:TPU:17, one launch (start us, length us, event | category | flops | bytes accessed | tf_op | source)
XLA Modules:
  0.0 93.1 jit_solution(15185346896679648169)
XLA Ops:
  0.0 1.3 %copy.6.counts = s32[1,4,2]{2,1,0:T(4,128)} copy(s32[1,4,2]{1,2,0:T(2,128)} %param.9) | data formatting | bytes 64 | tf_op args[4]
  1.3 89.3 %radial.1 = bf16[256,2560]{1,0:T(8,128)(2,1)} custom-call(bf16[256,2560]{1,0:T(8,128)(2,1)} %q_ref.1, bf16[256,2560]{1,0:T(8,128)(2,1)} %k_ref.1, bf16[256,2560]{1,0:T(8,128)(2,1)} %v_ref.1, s32[1,4,2,8]{3,2,1,0:T(2,128)} %lists.1, s32[1,4,2]{2,1,0:T(4,128)} %copy.6.counts), custom_call_target="tpu_custom_call" | custom-call | tf_op jit(solution)/shard_map/radial/pallas_call | solution.py:469
  90.6 2.5 %copy.8 = bf16[256,2560]{1,0:T(8,128)(2,1)} copy(bf16[256,2560]{1,0:T(8,128)(2,1)} %radial.1) | data formatting | bytes 2621440

commit v3 on v2

--- a/solution.py
+++ b/solution.py
@@ -235,6 +235,16 @@
         for i in range(1, n // HEAD):
             total = total + p[:, i * HEAD:(i + 1) * HEAD]
         return total
+
+    together = max(n for n in (1, 2, 3, 4, 5) if heads % n == 0)
+
+    def by_heads(one):
+        def step(i, carry):
+            for u in range(together):
+                one(together * i + u)
+            return carry
+
+        lax.fori_loop(0, heads // together, step, 0)
 
     def attend(keys, values, bias, first=False):
         def one(h):
@@ -264,15 +274,7 @@
                 acc[h] = acc[h] * factor + mixed
             top[h] = best
 
-        def step(i, carry):
-            one(2 * i)
-            one(2 * i + 1)
-            return carry
-
-        if heads % 2:
-            lax.fori_loop(0, heads, lambda i, c: (one(i), c)[1], 0)
-        else:
-            lax.fori_loop(0, heads // 2, step, 0)
+        by_heads(one)
 
     def put_inner(kv, cols, x):
         inner[kv, :, cols] = x
@@ -401,19 +403,18 @@
 
         @pl.when(has_out)
         def _():
-            pass_cross(2)
             for kv in range(2):
                 pack_copy(kv).wait_recv()
             attend_outer()
+            pass_cross(2)
             attend_big()
 
-    def finish(h, carry):
+    def finish(h):
         cols = pl.ds(pl.multiple_of(h * HEAD, HEAD), HEAD)
         total = jnp.sum(tot[h], axis=1, keepdims=True)
         out_ref[:, cols] = (acc[h] / total).astype(out_ref.dtype)
-        return carry
-
-    lax.fori_loop(0, heads, finish, 0)
+
+    by_heads(finish)
 
     for slot, p, ok in sends_list:
         @pl.when(ok)

time: 94.7 us -> 86.5 us (0.913); the launches traced: 93.1 us -> 86.3 us
  Pallas kernels: 89.3 us -> 82.5 us
    pallas_call x1, Pallas kernels: 89.3 us -> 82.5 us  [shards(): pl.pallas_call(functools.partial(body, n_ctx, nblk), out_shape=jax.ShapeD...]
where the time goes in v3:
time: 86.5 us; the launch traced here: 86.3 us
  Pallas kernels  82.5 us (95%)
  local copies, waits for them, and re-layouts  3.79 us (4%)
    pallas_call x1, Pallas kernels, shards(): pl.pallas_call(functools.partial(body, n_ctx, nblk), out_shape=jax.ShapeD...  82.5 us
    unnamed x2, local copies, waits for them, and re-layouts  3.79 us

profile of v3, /device:TPU:17, one launch (start us, length us, event | category | flops | bytes accessed | tf_op | source)
XLA Modules:
  0.0 86.3 jit_solution(11921015354914460129)
XLA Ops:
  0.0 1.3 %copy.6.counts = s32[1,4,2]{2,1,0:T(4,128)} copy(s32[1,4,2]{1,2,0:T(2,128)} %param.9) | data formatting | bytes 64 | tf_op args[4]
  1.3 82.5 %radial.1 = bf16[256,2560]{1,0:T(8,128)(2,1)} custom-call(bf16[256,2560]{1,0:T(8,128)(2,1)} %q_ref.1, bf16[256,2560]{1,0:T(8,128)(2,1)} %k_ref.1, bf16[256,2560]{1,0:T(8,128)(2,1)} %v_ref.1, s32[1,4,2,8]{3,2,1,0:T(2,128)} %lists.1, s32[1,4,2]{2,1,0:T(4,128)} %copy.6.counts), custom_call_target="tpu_custom_call" | custom-call | tf_op jit(solution)/shard_map/radial/pallas_call | solution.py:470
  83.9 2.5 %copy.8 = bf16[256,2560]{1,0:T(8,128)(2,1)} copy(bf16[256,2560]{1,0:T(8,128)(2,1)} %radial.1) | data formatting | bytes 2621440

commit v4 on v3

--- a/solution.py
+++ b/solution.py
@@ -16,12 +16,19 @@
 
 def body(
     n_ctx, nblk,
-    q_ref, k_ref, v_ref, lists, counts, out_ref,
+    q_hbm, k_hbm, v_hbm, lists, counts, out_ref,
+    q_ref, k_ref, v_ref,
     near, forwarded, big, inner, outer, far, far_pack, relay_pack, hop, pick_near, pick_far, got_near, got_far,
     acc, top, tot,
     s_list, s_near, s_full, s_far, s_relay, s_fwd, s_pack, s_hop,
-    r_list, r_near, r_big, r_far, r_fwd, r_outer, r_hop,
+    r_list, r_near, r_big, r_far, r_fwd, r_outer, r_hop, r_own,
 ):
+    own = [
+        pltpu.make_async_copy(src, dst, r_own.at[i])
+        for i, (src, dst) in enumerate(((k_hbm, k_ref), (v_hbm, v_ref), (q_hbm, q_ref)))
+    ]
+    for copy in own:
+        copy.start()
     rows, width = q_ref.shape
     heads = width // HEAD
     bs = rows // nblk
@@ -127,12 +134,12 @@
 
     def near_copy(c):
         kv, r = part(c)
-        return remote((k_ref, v_ref)[kv].at[r], near.at[kv, r], s_near.at[c], r_near.at[c], twin)
+        return remote((k_hbm, v_hbm)[kv].at[r], near.at[kv, r], s_near.at[c], r_near.at[c], twin)
 
     def cross_copy(c):
         kv, r = part(c)
         return remote(
-            (k_ref, v_ref)[kv].at[r], big.at[0, kv, r], s_full.at[0, c], r_big.at[0, c], d + s
+            (k_hbm, v_hbm)[kv].at[r], big.at[0, kv, r], s_full.at[0, c], r_big.at[0, c], d + s
         )
 
     def twin_copy(c):
@@ -160,7 +167,7 @@
 
     def hop_copy():
         kv, r = part(CHUNKS - 1)
-        return remote((k_ref, v_ref)[kv].at[r], hop, s_hop.at[0], r_hop, d - 4 * s)
+        return remote((k_hbm, v_hbm)[kv].at[r], hop, s_hop.at[0], r_hop, d - 4 * s)
 
     def hop_on_copy():
         kv, r = part(CHUNKS - 1)
@@ -181,6 +188,9 @@
     @pl.when(gets_relay)
     def _():
         hop_copy().start()
+
+    for copy in own:
+        copy.wait()
 
     for slot, p, ok in has_list:
         @pl.when(ok)
@@ -214,13 +224,13 @@
         block = lax.broadcasted_iota(jnp.int32, (1, rows), 1) // bs
         seen = jnp.zeros((1, rows), jnp.int32)
         for j in range(nblk):
-            hit = (block == lists[0, 0, side, j]) & (jnp.full((1, rows), j) < counts[0, 0, side])
+            hit = (block == lists[0, 0, side, j]) & (jnp.full((1, rows), j) < counts[0, side, 0])
             seen = seen + hit.astype(jnp.int32)
         return as_bias(seen > 0)
 
     def listed_bias(side):
         column = lax.broadcasted_iota(jnp.int32, (1, cap1 * bs), 1)
-        return as_bias(column < counts[0, 1, side] * bs)
+        return as_bias(column < counts[0, side, 1] * bs)
 
     def wide(x, n):
         k = n // HEAD
@@ -347,7 +357,7 @@
     column = lax.broadcasted_iota(jnp.int32, (1, sum(far_rows) + spare), 1)
     limit = jnp.zeros(column.shape, jnp.int32)
     for i in range(4):
-        end = far_start[i] + counts[0, 2 + i // 2, i % 2] * bs
+        end = far_start[i] + counts[0, i % 2, 2 + i // 2] * bs
         limit = jnp.where(column >= far_start[i], end, limit)
     limit = jnp.where(column >= sum(far_rows), 0, limit)
     far_bias = as_bias(column < limit)
@@ -465,14 +475,18 @@
     far_room = far_rows + (-far_rows) % HEAD
     kv = jnp.bfloat16
     vmem = pl.BlockSpec(memory_space=pltpu.VMEM)
+    hbm = pl.BlockSpec(memory_space=pl.ANY)
     smem = pl.BlockSpec(memory_space=pltpu.SMEM)
     dma = pltpu.SemaphoreType.DMA
     return pl.pallas_call(
         functools.partial(body, n_ctx, nblk),
         out_shape=jax.ShapeDtypeStruct((rows, width), jnp.bfloat16),
-        in_specs=[vmem, vmem, vmem, smem, smem],
+        in_specs=[hbm, hbm, hbm, smem, smem],
         out_specs=vmem,
         scratch_shapes=[
+            pltpu.VMEM((rows, width), kv),
+            pltpu.VMEM((rows, width), kv),
+            pltpu.VMEM((rows, width), kv),
             pltpu.VMEM((2, rows, width), kv),
             pltpu.VMEM((2, rows, width), kv),
             pltpu.VMEM((2, 2, rows, width), kv),
@@ -490,13 +504,13 @@
             pltpu.VMEM((heads, rows, HEAD), jnp.float32),
             pltpu.VMEM((heads, rows, HEAD), jnp.float32),
             dma((5,)), dma((CHUNKS,)), dma((2, CHUNKS)), dma((4,)), dma((CHUNKS,)), dma((CHUNKS,)), dma((2,)), dma((2,)),
-            dma((5,)), dma((CHUNKS,)), dma((2, CHUNKS)), dma((4,)), dma((CHUNKS,)), dma((2,)), dma,
+            dma((5,)), dma((CHUNKS,)), dma((2, CHUNKS)), dma((4,)), dma((CHUNKS,)), dma((2,)), dma, dma((3,)),
         ],
         compiler_params=pltpu.CompilerParams(
             collective_id=0, has_side_effects=True, vmem_limit_bytes=60 * 1024 * 1024
         ),
         name="radial",
-    )(queries, keys, values, kv_lists, kv_counts)
+    )(queries, keys, values, kv_lists, jnp.swapaxes(kv_counts, 1, 2))
 
 
 def solution(mesh):

time: 86.5 us -> 84 us (0.971)
  local copies, waits for them, and re-layouts: 3.79 us -> 2.46 us
  Pallas kernels: 82.5 us -> 81.4 us
    unnamed x2 -> x1, local copies, waits for them, and re-layouts: 3.79 us -> 2.46 us
    pallas_call x1, Pallas kernels: 82.5 us -> 81.4 us  [shards(): pl.pallas_call(functools.partial(body, n_ctx, nblk), out_shape=jax.ShapeD...]
where the time goes in v4:
time: 84 us; the launch traced here: 83.8 us
  Pallas kernels  81.4 us (97%)
  local copies, waits for them, and re-layouts  2.46 us (3%)
    pallas_call x1, Pallas kernels, shards(): pl.pallas_call(functools.partial(body, n_ctx, nblk), out_shape=jax.ShapeD...  81.4 us
    unnamed x1, local copies, waits for them, and re-layouts  2.46 us

profile of v4, /device:TPU:17, one launch (start us, length us, event | category | flops | bytes accessed | tf_op | source)
XLA Modules:
  0.0 83.8 jit_solution(4143283190705454960)
XLA Ops:
  0.0 81.4 %radial.1 = bf16[256,2560]{1,0:T(8,128)(2,1)} custom-call(bf16[256,2560]{1,0:T(8,128)(2,1)} %q_hbm.1, bf16[256,2560]{1,0:T(8,128)(2,1)} %k_hbm.1, bf16[256,2560]{1,0:T(8,128)(2,1)} %v_hbm.1, s32[1,4,2,8]{3,2,1,0:T(2,128)} %lists.1, s32[1,2,4]{2,1,0:T(2,128)} %bitcast.1), custom_call_target="tpu_custom_call" | custom-call | tf_op jit(solution)/shard_map/radial/pallas_call | solution.py:481
  81.4 2.5 %copy.7 = bf16[256,2560]{1,0:T(8,128)(2,1)} copy(bf16[256,2560]{1,0:T(8,128)(2,1)} %radial.1) | data formatting | bytes 2621440
